TPU v7x, 32 devices: a whole 2x2x4 slice. The times are simulated.
32 devices in a mesh: rep: 4 (over z), fsdp: 8 (over y, x, core).
Axes of the slice: x: 2, y: 2, z: 4, core: 2. Of those that a mesh axis runs over, the one named last changes fastest.
Arguments:
- tokens: bfloat16 [4096, 3072], P(('rep', 'fsdp')), may hold values from -6 to 6
- gate_saved: bfloat16 [4096, 8192], P('rep', 'fsdp'), may hold values from -6 to 6
- up_saved: bfloat16 [4096, 8192], P('rep', 'fsdp'), may hold values from -6 to 6
- hidden_grad: bfloat16 [4096, 8192], P('rep', 'fsdp'), may hold values from -6 to 6
- gate_num: bfloat16 [4, 3072, 8192], P('rep', None, 'fsdp'), may hold values from -6 to 6
- up_num: bfloat16 [4, 3072, 8192], P('rep', None, 'fsdp'), may hold values from -6 to 6
- push_weight: bfloat16 [4], P('rep'), may hold values from 0.5 to 2
- step: int32 [1], replicated, may hold values from 0 to 15
Outputs:
- input_grad: bfloat16 [4096, 3072], P(('rep', 'fsdp'))
- gate_next: bfloat16 [4, 3072, 8192], P('rep', None, 'fsdp')
- up_next: bfloat16 [4, 3072, 8192], P('rep', None, 'fsdp')
- weight_next: float32 [4], P('rep')
All inputs are finite; a program needn't handle non-finite values.
Results may differ from a plain program's by a relative error of at most 0.017.
Values may be sent and summed in bfloat16 or wider, within the bound.
A program may use at most 192 MiB of HBM per device.

v0:
```python
from functools import partial

import jax
import jax.numpy as jnp
from jax import lax
from jax.experimental import pallas as pl
from jax.experimental.pallas import tpu as pltpu
from jax.sharding import PartitionSpec as P


MESH = pl.DeviceIdType.MESH
ANY = pl.BlockSpec(memory_space=pl.ANY)
VMEM = pl.BlockSpec(memory_space=pltpu.VMEM)
SPLITS = (3, 5, 13, 3)


def greet(me, n):
    barrier = pltpu.get_barrier_semaphore()
    for k in range(1, n):
        pl.semaphore_signal(
            barrier, inc=1, device_id={"fsdp": lax.rem(me + k, n)}, device_id_type=MESH
        )
    pl.semaphore_wait(barrier, n - 1)


def gather_body(n, tok, out, sems, between=None):
    send, recv, fsend, frecv, local = sems
    me = lax.axis_index("fsdp")
    rows = tok.shape[0]
    beside = me + 1 - 2 * lax.rem(me, 2)

    def block(owner):
        return out.at[pl.ds(pl.multiple_of(owner * rows, rows), rows), :]

    def remote(src, owner, s, r, target):
        return pltpu.make_async_remote_copy(
            src_ref=src,
            dst_ref=block(owner),
            send_sem=s,
            recv_sem=r,
            device_id={"fsdp": target},
            device_id_type=MESH,
        )

    greet(me, n)
    direct = []
    for k in range(1, n // 2):
        copy = remote(tok, me, send.at[k], recv.at[k], lax.rem(me + 2 * k, n))
        copy.start()
        direct.append(copy)
    near = remote(tok, me, send.at[0], recv.at[0], beside)
    near.start()
    own = pltpu.make_async_copy(tok, block(me), local.at[0])
    own.start()
    if between is not None:
        between()
    relays = []
    for k in range(1, n // 2):
        owner = lax.rem(me + n - 2 * k, n)
        remote(tok, owner, send.at[k], recv.at[k], beside).wait_recv()
        copy = remote(block(owner), owner, fsend.at[k], frecv.at[k], beside)
        copy.start()
        relays.append(copy)
    own.wait()
    near.wait_send()
    remote(tok, beside, send.at[0], recv.at[0], beside).wait_recv()
    for copy in direct:
        copy.wait_send()
    for k in range(1, n // 2):
        relays[k - 1].wait_send()
        owner = lax.rem(beside + n - 2 * k, n)
        remote(tok, owner, fsend.at[k], frecv.at[k], beside).wait_recv()


def first_kernel(n, tok, gate, up, cot, out, gate_delta, up_delta, *sems):
    rows = gate.shape[0]
    tile = min(32, rows)

    def deltas():
        @pl.loop(0, rows // tile)
        def _(i):
            at = pl.ds(pl.multiple_of(i * tile, tile), tile)
            g = gate[at, :].astype(jnp.float32)
            u = up[at, :].astype(jnp.float32)
            h = cot[at, :].astype(jnp.float32)
            p = jax.nn.sigmoid(g)
            hp = h * p
            gate_delta[at, :] = (hp * u * (1.0 + g * (1.0 - p))).astype(jnp.bfloat16)
            up_delta[at, :] = (hp * g).astype(jnp.bfloat16)

    gather_body(n, tok, out, sems, deltas)


def rest_kernel(n, tok, after, out, *sems):
    gather_body(n, tok, out, sems)


def gather_sems(n):
    return [pltpu.SemaphoreType.DMA((n // 2,))] * 4 + [pltpu.SemaphoreType.DMA((1,))]


def first_call(n, tok, gate, up, cot):
    like = jax.ShapeDtypeStruct(gate.shape, jnp.bfloat16)
    return pl.pallas_call(
        partial(first_kernel, n),
        name="first_gather",
        out_shape=(jax.ShapeDtypeStruct((n * tok.shape[0], tok.shape[1]), tok.dtype), like, like),
        in_specs=[VMEM] * 4,
        out_specs=(ANY, VMEM, VMEM),
        scratch_shapes=gather_sems(n),
        compiler_params=pltpu.CompilerParams(collective_id=0, has_side_effects=True),
    )(tok, gate, up, cot)


def rest_call(n, ident, tok, after):
    return pl.pallas_call(
        partial(rest_kernel, n),
        name="rest_gather",
        out_shape=jax.ShapeDtypeStruct((n * tok.shape[0], tok.shape[1]), tok.dtype),
        in_specs=[VMEM, ANY],
        out_specs=ANY,
        scratch_shapes=gather_sems(n),
        compiler_params=pltpu.CompilerParams(collective_id=ident, has_side_effects=True),
        cost_estimate=pl.CostEstimate(flops=0, bytes_accessed=100_000_000, transcendentals=0),
    )(tok, after)


def scatter_kernel(n, term, out, parts, send, recv):
    me = lax.axis_index("fsdp")
    rows = out.shape[0]

    def block(owner):
        return term.at[pl.ds(pl.multiple_of(owner * rows, rows), rows), :]

    greet(me, n)
    own = pltpu.make_async_copy(block(me), parts.at[0], recv.at[0])
    own.start()
    copies = []
    for k in range(1, n):
        peer = lax.rem(me + k, n)
        copy = pltpu.make_async_remote_copy(
            src_ref=block(peer),
            dst_ref=parts.at[k],
            send_sem=send.at[k],
            recv_sem=recv.at[k],
            device_id={"fsdp": peer},
            device_id_type=MESH,
        )
        copy.start()
        copies.append(copy)
    own.wait()
    for copy in copies:
        copy.wait()
    tile = min(16, rows)

    @pl.loop(0, rows // tile)
    def _(i):
        at = pl.ds(pl.multiple_of(i * tile, tile), tile)
        total = parts[0, at, :].astype(jnp.float32)
        for k in range(1, n):
            total = total + parts[k, at, :].astype(jnp.float32)
        out[at, :] = total.astype(out.dtype)


def scatter_call(n, ident, term):
    rows, cols = term.shape[0] // n, term.shape[1]
    return pl.pallas_call(
        partial(scatter_kernel, n),
        name="grad_scatter",
        out_shape=jax.ShapeDtypeStruct((rows, cols), term.dtype),
        in_specs=[ANY],
        out_specs=VMEM,
        scratch_shapes=[
            pltpu.VMEM((n, rows, cols), term.dtype),
            pltpu.SemaphoreType.DMA((n,)),
            pltpu.SemaphoreType.DMA((n,)),
        ],
        compiler_params=pltpu.CompilerParams(collective_id=ident, has_side_effects=True),
        cost_estimate=pl.CostEstimate(flops=0, bytes_accessed=200_000_000, transcendentals=0),
    )(term)


def average(own, peer):
    return 0.5 * (own.astype(jnp.float32) + peer.astype(jnp.float32))


def mix_kernel(first, *refs):
    refs = list(refs)
    parts, rest = refs[:4], refs[4:]
    if first:
        grad = rest.pop(0)
    else:
        rest = rest[3:]
    for at in range(2):
        out = rest.pop(0)
        out[...] = average(parts[2 * at][...], parts[2 * at + 1][...]).astype(out.dtype)
    if first:
        rest.pop(0)[...] = grad[...]


def mix_call(parts, whole, low, tile, grad, mixed=None):
    rows, cols = parts[0].shape
    part = pl.BlockSpec((tile, cols), lambda i: (i, 0))
    held = pl.BlockSpec((tile, cols), lambda i: (low // tile + i, 0))
    first = mixed is None
    out = jax.ShapeDtypeStruct((whole, cols), parts[0].dtype)
    operands, in_specs = list(parts), [part] * 4
    out_shape, out_specs = [out, out], [held, held]
    if first:
        all_of = pl.BlockSpec(grad.shape, lambda i: (0, 0))
        operands.append(grad)
        in_specs.append(all_of)
        out_shape.append(jax.ShapeDtypeStruct(grad.shape, grad.dtype))
        out_specs.append(all_of)
    else:
        operands += [grad, *mixed]
        in_specs += [ANY] * 3
    return pl.pallas_call(
        partial(mix_kernel, first),
        name="mix",
        grid=(rows // tile,),
        out_shape=out_shape,
        in_specs=in_specs,
        out_specs=out_specs,
        input_output_aliases={} if first else {5: 0, 6: 1},
        cost_estimate=pl.CostEstimate(
            flops=4 * rows * cols, bytes_accessed=12 * rows * cols, transcendentals=0
        ),
    )(*operands)


def halves(shard_rows, delta, num, factor):
    total = lax.dot_general(
        shard_rows, delta, (((0,), (0,)), ((), ())), preferred_element_type=jnp.float32
    )
    grad = (factor * total).astype(jnp.bfloat16)
    return (num.astype(jnp.float32) - grad.astype(jnp.float32)).astype(jnp.bfloat16)


def exchange(args, exponent):
    return exchange_at(args, exponent)


def exchange_at(args, exponent):
    tokens, gate_num, up_num, push_weight, gate_delta, up_delta, gate_first, up_first = args
    n = lax.axis_size("fsdp")
    peers = lax.axis_size("rep")
    perm = [(i, (i + (1 << exponent)) % peers) for i in range(peers)]
    depth = tokens.shape[1]
    factor = depth ** (-0.5)
    unit = depth // sum(SPLITS)
    bounds = [0]
    for share in SPLITS:
        bounds.append(bounds[-1] + share * unit)

    def send(value):
        return lax.ppermute(value, "rep", perm)

    own = [(gate_first, up_first)]
    got = [(send(gate_first), send(up_first))]
    rest = rest_call(n, 1 + 2 * exponent, tokens[:, bounds[1] :], gate_first)
    for low, high in zip(bounds[1:-1], bounds[2:]):
        rows = rest[:, low - bounds[1] : high - bounds[1]]
        own.append(
            (
                halves(rows, gate_delta, gate_num[low:high], factor),
                halves(rows, up_delta, up_num[low:high], factor),
            )
        )
        at = len(got)
        got.append((send(own[-1][0]), send(own[-1][1])))
    peer_weight = send(push_weight)
    weight = push_weight[0].astype(jnp.float32)
    gate_point = (gate_num.astype(jnp.float32) / weight).astype(jnp.bfloat16)
    up_point = (up_num.astype(jnp.float32) / weight).astype(jnp.bfloat16)
    contract_cols = (((1,), (1,)), ((), ()))
    term = factor * (
        lax.dot_general(gate_delta, gate_point, contract_cols, preferred_element_type=jnp.float32)
        + lax.dot_general(up_delta, up_point, contract_cols, preferred_element_type=jnp.float32)
    )
    input_grad = scatter_call(n, 2 + 2 * exponent, term.astype(jnp.bfloat16))
    mixed = None
    for at, low in enumerate(bounds[:-1]):
        parts = (own[at][0], got[at][0], own[at][1], got[at][1])
        if at == 0:
            *mixed, grad_out = mix_call(parts, depth, low, unit, input_grad)
        else:
            mixed = mix_call(parts, depth, low, unit, input_grad, mixed)
    weight_next = 0.5 * (push_weight.astype(jnp.float32) + peer_weight.astype(jnp.float32))
    return grad_out, mixed[0][None], mixed[1][None], weight_next


def shards(tokens, gate_saved, up_saved, hidden_grad, gate_num, up_num, push_weight, step):
    n = lax.axis_size("fsdp")
    levels = lax.axis_size("rep").bit_length() - 1
    chosen = step[0] % levels
    depth = tokens.shape[1]
    factor = depth ** (-0.5)
    first = depth // sum(SPLITS) * SPLITS[0]
    rows, gate_delta, up_delta = first_call(
        n, tokens[:, :first], gate_saved, up_saved, hidden_grad
    )
    gate_first = halves(rows, gate_delta, gate_num[0, :first], factor)
    up_first = halves(rows, up_delta, up_num[0, :first], factor)
    args = (
        tokens, gate_num[0], up_num[0], push_weight, gate_delta, up_delta, gate_first, up_first
    )
    branches = [partial(exchange, exponent=exponent) for exponent in range(levels)]
    return lax.switch(chosen, branches, args)


def solution(mesh):
    return jax.shard_map(
        shards,
        mesh=mesh,
        in_specs=(
            P(("rep", "fsdp"), None),
            P("rep", "fsdp"),
            P("rep", "fsdp"),
            P("rep", "fsdp"),
            P("rep", None, "fsdp"),
            P("rep", None, "fsdp"),
            P("rep"),
            P(),
        ),
        out_specs=(
            P(("rep", "fsdp"), None),
            P("rep", None, "fsdp"),
            P("rep", None, "fsdp"),
            P("rep"),
        ),
        check_vma=False,
    )
```

profile of v0, /device:TPU:0, one launch (start us, length us, event | category | flops | bytes accessed | tf_op | source)
XLA Modules:
  0.0 321.8 jit_solution(174006791610335644)
XLA Ops:
  1.3 1.5 slice.70.tok
  2.8 16.2 %first_gather.1 = (bf16[1024,384]{1,0:T(8,128)(2,1)}, bf16[1024,1024]{1,0:T(8,128)(2,1)}, bf16[1024,1024]{1,0:T(8,128)(2,1)}) custom-call(bf16[128,384]{1,0:T(8,128)(2,1)} %slice.70.tok, bf16[1024,1024]{1,0:T(8,128)(2,1)} %gate.1, bf16[1024,1024]{1,0:T(8,128)(2,1)} %up.1, bf16[1024,1024]{1,0:T(8,128)(2,1)} %cot.1), custom_call_target="tpu_custom_call" | custom-call | tf_op jit(solution)/shard_map/first_gather/pallas_call | solution.py:104
  19.1 3.1 fusion.54
  22.2 2.8 fusion.55
  25.0 295.6 %conditional.1 = (bf16[128,3072]{1,0:T(8,128)(2,1)}, bf16[1,3072,1024]{2,1,0:T(8,128)(2,1)}, bf16[1,3072,1024]{2,1,0:T(8,128)(2,1)}, f32[1]{0:T(128)}) conditional(s32[]{:T(128)} %clamp.3, (bf16[384,1024]{1,0:T(8,128)(2,1)S(1)}, bf16[384,1024]{1,0:T(8,128)(2,1)S(1)}, bf16[1,3072,1024]{2,1,0:T(8,128)(2,1)}, bf16[1]{0:T(256)(128)(2,1)}, ...), branch_computations={%region_0.1_spmd, %region_1.2_spmd} | conditional | flops 24233115648 | bytes 573482496 | solution.py:309
  25.1 1.6 collective-permute-start
  26.7 1.6 collective-permute-start.1
  28.3 0.9 slice.47.tok
  29.2 37.7 %rest_gather.2 = bf16[1024,2688]{1,0:T(8,128)(2,1)} custom-call(bf16[128,2688]{1,0:T(8,128)(2,1)} %slice.47.tok, bf16[384,1024]{1,0:T(8,128)(2,1)S(1)} %get-tuple-element.32.refs_0_.after), custom_call_target="tpu_custom_call" | custom-call | bytes 100000000 | tf_op jit(solution)/shard_map/cond/branch_0_fun/rest_gather/pallas_call | solution.py:116
  66.9 4.1 %fusion.20.refs_0_ = bf16[640,1024]{1,0:T(8,128)(2,1)S(1)} fusion(bf16[1,3072,1024]{2,1,0:T(8,128)(2,1)} %get-tuple-element.79, bf16[1024,1024]{1,0:T(8,128)(2,1)} %get-tuple-element.36, bf16[1024,2688]{1,0:T(8,128)(2,1)} %rest_gather.2), kind=kOutput, calls=%fused_computation.21 | convolution fusion | flops 1346109440 | bytes 6029312 | tf_op jit(solution)/shard_map/cond/branch_0_fun/dot_general | solution.py:233
  71.1 1.6 collective-permute-start.6
  72.7 7.0 %fusion.1.refs_0_ = bf16[1664,1024]{1,0:T(8,128)(2,1)} fusion(bf16[1,3072,1024]{2,1,0:T(8,128)(2,1)} %get-tuple-element.79, bf16[1024,1024]{1,0:T(8,128)(2,1)S(1)} %copy-done.4, bf16[1024,2688]{1,0:T(8,128)(2,1)S(1)} %copy-done), kind=kOutput, calls=%fused_computation.6 | convolution fusion | flops 3499884544 | bytes 12320768 | tf_op jit(solution)/shard_map/cond/branch_0_fun/dot_general | solution.py:233
  79.7 1.1 collective-permute-start.4
  80.8 0.6 collective-permute-start.8
  82.2 9.2 %fusion.4 = f32[3072,1024]{0,1:T(8,128)} fusion(bf16[1024,1024]{1,0:T(8,128)(2,1)S(1)} %copy-done.4, bf16[1,3072,1024]{2,1,0:T(8,128)(2,1)S(1)} %bitcast.97, f32[]{:T(128)} %bitcast), kind=kOutput, calls=%fused_computation.11 | convolution fusion | flops 6451888128 | bytes 20971524 | tf_op jit(solution)/shard_map/cond/branch_0_fun/dot_general | solution.py:278
  91.5 5.5 %fusion.refs_2_ = bf16[1664,1024]{1,0:T(8,128)(2,1)} fusion(bf16[1,3072,1024]{2,1,0:T(8,128)(2,1)S(1)} %bitcast.101, bf16[1024,1024]{1,0:T(8,128)(2,1)S(1)} %copy-done.6, bf16[1024,2688]{1,0:T(8,128)(2,1)S(1)} %copy-done), kind=kOutput, calls=%fused_computation.4 | convolution fusion | flops 3499884544 | bytes 12320768 | tf_op jit(solution)/shard_map/cond/branch_0_fun/dot_general | solution.py:233
  97.0 2.7 fusion.19.refs_2_
  99.6 1.9 fusion.22.refs_0_
  101.5 75.6 %collective-permute-done.8 = bf16[1]{0:T(256)(128)(2,1)} collective-permute-done((bf16[1]{0:T(256)(128)(2,1)}, bf16[1]{0:T(256)(128)(2,1)}, u32[]{:S(2)}, u32[]{:S(2)}) %collective-permute-start.8) | collective-permute-done | bytes 34 | tf_op jit(solution)/shard_map/cond/branch_0_fun/ppermute | solution.py:257
  177.2 1.9 fusion.21.refs_2_
  179.1 1.5 collective-permute-start.2
  180.7 1.0 copy-done.10
  181.7 3.4 %collective-permute-start.3 = (bf16[384,1024]{1,0:T(8,128)(2,1)}, bf16[384,1024]{1,0:T(8,128)(2,1)S(1)}, u32[]{:S(2)}, u32[]{:S(2)}) collective-permute-start(bf16[384,1024]{1,0:T(8,128)(2,1)} %fusion.21.refs_2_), channel_id=1, source_target_pairs={{0,8},{8,16},{16,24},{24,0},{1,9},{9,17},{17,25},{25,1},{2,10},{10... | collective-permute-start | bytes 2359304 | tf_op jit(solution)/shard_map/cond/branch_0_fun/ppermute | solution.py:257
  185.1 11.4 %fusion.2.term = bf16[1024,3072]{1,0:T(8,128)(2,1)} fusion(f32[3072,1024]{0,1:T(8,128)} %fusion.4, bf16[1024,1024]{1,0:T(8,128)(2,1)S(1)} %copy-done.6, bf16[1,3072,1024]{2,1,0:T(8,128)(2,1)S(1)} %bitcast.101, f32[]{:T(128)} %bitcast), kind=kOutput, calls=%fused_computation.9 | convolution fusion | flops 6461325312 | bytes 27262980 | tf_op jit(solution)/shard_map/cond/branch_0_fun/dot_general | solution.py:279
  196.5 71.6 %grad_scatter.2.refs_4_ = bf16[128,3072]{1,0:T(8,128)(2,1)} custom-call(bf16[1024,3072]{1,0:T(8,128)(2,1)} %fusion.2.term), custom_call_target="tpu_custom_call" | custom-call | bytes 200000000 | tf_op jit(solution)/shard_map/cond/branch_0_fun/grad_scatter/pallas_call | solution.py:167
  269.4 4.0 %mix.8 = (bf16[3072,1024]{1,0:T(8,128)(2,1)}, bf16[3072,1024]{1,0:T(8,128)(2,1)}, bf16[128,3072]{1,0:T(8,128)(2,1)}) custom-call(bf16[384,1024]{1,0:T(8,128)(2,1)S(1)} %get-tuple-element.32.refs_0_.after, bf16[384,1024]{1,0:T(8,128)(2,1)} %collective-permute-done.refs_1_, bf16[384,1024]{1,0:T(8,128)(2,1)S(1)} %get-tuple-element.33.refs_2_, ...), custom_call_target="tpu_custom_call" | custom-call | flops 1572864 | bytes 4718592 | tf_op jit(solution)/shard_map/cond/branch_0_fun/mix/pallas_call | solution.py:218
  273.4 10.6 %collective-permute-done.7.refs_3_ = bf16[640,1024]{1,0:T(8,128)(2,1)} collective-permute-done((bf16[640,1024]{1,0:T(8,128)(2,1)}, bf16[640,1024]{1,0:T(8,128)(2,1)}, u32[]{:S(2)}, u32[]{:S(2)}) %collective-permute-start.7) | collective-permute-done | bytes 1310752 | tf_op jit(solution)/shard_map/cond/branch_0_fun/ppermute | solution.py:257
  284.0 5.4 %mix.9 = (bf16[3072,1024]{1,0:T(8,128)(2,1)}, bf16[3072,1024]{1,0:T(8,128)(2,1)}) custom-call(bf16[640,1024]{1,0:T(8,128)(2,1)} %copy-done.8, bf16[640,1024]{1,0:T(8,128)(2,1)} %copy-done.10, bf16[640,1024]{1,0:T(8,128)(2,1)} %fusion.19.refs_2_, bf16[640,1024]{1,0:T(8,128)(2,1)} %collective-permute-done.7.refs_3_, ...), custom_call_target="tpu_custom_call", output_to_operand_aliasing={{0}: (5, {}), {1}: (6, {})} | custom-call | flops 2621440 | bytes 7864320 | tf_op jit(solution)/shard_map/cond/branch_0_fun/mix/pallas_call | solution.py:218
  289.4 11.8 %mix.10 = (bf16[3072,1024]{1,0:T(8,128)(2,1)}, bf16[3072,1024]{1,0:T(8,128)(2,1)}) custom-call(bf16[1664,1024]{1,0:T(8,128)(2,1)} %fusion.1.refs_0_, bf16[1664,1024]{1,0:T(8,128)(2,1)} %collective-permute-done.4.refs_1_, bf16[1664,1024]{1,0:T(8,128)(2,1)} %fusion.refs_2_, ...), custom_call_target="tpu_custom_call", output_to_operand_aliasing={{0}: (5, {}), {1}: (6, {})} | custom-call | flops 6815744 | bytes 20447232 | tf_op jit(solution)/shard_map/cond/branch_0_fun/mix/pallas_call | solution.py:218
  301.2 14.8 %collective-permute-done.3.refs_3_ = bf16[384,1024]{1,0:T(8,128)(2,1)S(1)} collective-permute-done((bf16[384,1024]{1,0:T(8,128)(2,1)}, bf16[384,1024]{1,0:T(8,128)(2,1)S(1)}, u32[]{:S(2)}, u32[]{:S(2)}) %collective-permute-start.3) | collective-permute-done | bytes 786464 | tf_op jit(solution)/shard_map/cond/branch_0_fun/ppermute | solution.py:257
  316.0 0.9 copy-done.12
  316.9 3.8 %mix.11 = (bf16[3072,1024]{1,0:T(8,128)(2,1)}, bf16[3072,1024]{1,0:T(8,128)(2,1)}) custom-call(bf16[384,1024]{1,0:T(8,128)(2,1)} %fusion.22.refs_0_, bf16[384,1024]{1,0:T(8,128)(2,1)} %collective-permute-done.2.refs_1_, bf16[384,1024]{1,0:T(8,128)(2,1)} %fusion.21.refs_2_, ...), custom_call_target="tpu_custom_call", output_to_operand_aliasing={{0}: (5, {}), {1}: (6, {})} | custom-call | flops 1572864 | bytes 4718592 | tf_op jit(solution)/shard_map/cond/branch_0_fun/mix/pallas_call | solution.py:218
  (32 shorter events, 0.1 us)
Async XLA Ops:
  19.1 3.1 copy-start.2
  19.1 5.9 %copy-start.3 = (bf16[128,3072]{1,0:T(8,128)(2,1)S(1)}, bf16[128,3072]{1,0:T(8,128)(2,1)}, u32[]{:S(2)}) copy-start(bf16[128,3072]{1,0:T(8,128)(2,1)} %param.10) | copy-start | bytes 2359300
  25.1 154.0 %collective-permute-start = (bf16[384,1024]{1,0:T(8,128)(2,1)S(1)}, bf16[384,1024]{1,0:T(8,128)(2,1)}, u32[]{:S(2)}, u32[]{:S(2)}) collective-permute-start(bf16[384,1024]{1,0:T(8,128)(2,1)S(1)} %get-tuple-element.32.refs_0_.after), channel_id=1, source_target_pairs={{0,8},{8,16},{16,24},{24,0},{1,9},{9,17},{17,25},{25,1},{2,10},{10... | collective-permute-start | bytes 2359304 | tf_op jit(solution)/shard_map/cond/branch_0_fun/ppermute | solution.py:257
  26.7 152.5 %collective-permute-start.1 = (bf16[384,1024]{1,0:T(8,128)(2,1)S(1)}, bf16[384,1024]{1,0:T(8,128)(2,1)}, u32[]{:S(2)}, u32[]{:S(2)}) collective-permute-start(bf16[384,1024]{1,0:T(8,128)(2,1)S(1)} %get-tuple-element.33.refs_2_), channel_id=1, source_target_pairs={{0,8},{8,16},{16,24},{24,0},{1,9},{9,17},{17,25},{25,1},{2,10},{10... | collective-permute-start | bytes 2359304 | tf_op jit(solution)/shard_map/cond/branch_0_fun/ppermute | solution.py:257
  66.9 5.8 %copy-start = (bf16[1024,2688]{1,0:T(8,128)(2,1)S(1)}, bf16[1024,2688]{1,0:T(8,128)(2,1)}, u32[]{:S(2)}) copy-start(bf16[1024,2688]{1,0:T(8,128)(2,1)} %rest_gather.2) | copy-start | bytes 16515076 | tf_op jit(solution)/shard_map/cond
  66.9 5.8 %copy-start.4 = (bf16[1024,1024]{1,0:T(8,128)(2,1)S(1)}, bf16[1024,1024]{1,0:T(8,128)(2,1)}, u32[]{:S(2)}) copy-start(bf16[1024,1024]{1,0:T(8,128)(2,1)} %get-tuple-element.36) | copy-start | bytes 6291460 | tf_op jit(solution)/shard_map/cond
  66.9 15.2 %slice-start = ((s8[6291456]{0:T(1024)(128)(4,1)}), s8[4194304]{0:T(1024)(128)(4,1)S(1)}, s32[]{:S(2)}) async-start(s8[6291456]{0:T(1024)(128)(4,1)} %bitcast.96), calls=%async_computation | async-start | bytes 8388608 | tf_op jit(solution)/shard_map/cond
  71.0 8.6 %copy-start.8 = (bf16[640,1024]{1,0:T(8,128)(2,1)}, bf16[640,1024]{1,0:T(8,128)(2,1)S(1)}, u32[]{:S(2)}) copy-start(bf16[640,1024]{1,0:T(8,128)(2,1)S(1)} %fusion.20.refs_0_) | copy-start | bytes 3932164 | tf_op jit(solution)/shard_map/cond
  71.0 11.1 %slice-start.1 = ((s8[6291456]{0:T(1024)(128)(4,1)}), s8[2097152]{0:T(1024)(128)(4,1)S(1)}, s32[]{:S(2)}) async-start(s8[6291456]{0:T(1024)(128)(4,1)} %bitcast.96), calls=%async_computation.1 | async-start | bytes 4194304 | tf_op jit(solution)/shard_map/cond
  71.1 109.6 %collective-permute-start.6 = (bf16[640,1024]{1,0:T(8,128)(2,1)S(1)}, bf16[640,1024]{1,0:T(8,128)(2,1)S(1)}, u32[]{:S(2)}, u32[]{:S(2)}) collective-permute-start(bf16[640,1024]{1,0:T(8,128)(2,1)S(1)} %fusion.20.refs_0_), channel_id=1, source_target_pairs={{0,8},{8,16},{16,24},{24,0},{1,9},{9,17},{17,25},{25,1},{2,10},{10... | collective-permute-start | bytes 3932168 | tf_op jit(solution)/shard_map/cond/branch_0_fun/ppermute | solution.py:257
  72.7 18.8 %slice-start.4 = ((s8[6291456]{0:T(1024)(128)(4,1)}), s8[4194304]{0:T(1024)(128)(4,1)S(1)}, s32[]{:S(2)}) async-start(s8[6291456]{0:T(1024)(128)(4,1)} %bitcast.100), calls=%async_computation.4 | async-start | bytes 8388608 | tf_op jit(solution)/shard_map/cond
  79.7 209.8 %collective-permute-start.4 = (bf16[1664,1024]{1,0:T(8,128)(2,1)}, bf16[1664,1024]{1,0:T(8,128)(2,1)}, u32[]{:S(2)}, u32[]{:S(2)}) collective-permute-start(bf16[1664,1024]{1,0:T(8,128)(2,1)} %fusion.1.refs_0_), channel_id=1, source_target_pairs={{0,8},{8,16},{16,24},{24,0},{1,9},{9,17},{17,25},{25,1},{2,10},{10... | collective-permute-start | bytes 10223624 | tf_op jit(solution)/shard_map/cond/branch_0_fun/ppermute | solution.py:257
  80.8 96.4 %collective-permute-start.8 = (bf16[1]{0:T(256)(128)(2,1)}, bf16[1]{0:T(256)(128)(2,1)}, u32[]{:S(2)}, u32[]{:S(2)}) collective-permute-start(bf16[1]{0:T(256)(128)(2,1)} %get-tuple-element.85), channel_id=1, source_target_pairs={{0,8},{8,16},{16,24},{24,0},{1,9},{9,17},{17,25},{25,1},{2,10},{10... | collective-permute-start | bytes 14 | tf_op jit(solution)/shard_map/cond/branch_0_fun/ppermute | solution.py:257
  82.2 9.3 %copy-start.6 = (bf16[1024,1024]{1,0:T(8,128)(2,1)S(1)}, bf16[1024,1024]{1,0:T(8,128)(2,1)}, u32[]{:S(2)}) copy-start(bf16[1024,1024]{1,0:T(8,128)(2,1)} %get-tuple-element.38) | copy-start | bytes 6291460 | tf_op jit(solution)/shard_map/cond
  82.2 9.3 %slice-start.5 = ((s8[6291456]{0:T(1024)(128)(4,1)}), s8[2097152]{0:T(1024)(128)(4,1)S(1)}, s32[]{:S(2)}) async-start(s8[6291456]{0:T(1024)(128)(4,1)} %bitcast.100), calls=%async_computation.5 | async-start | bytes 4194304 | tf_op jit(solution)/shard_map/cond
  177.2 112.2 %collective-permute-start.5 = (bf16[1664,1024]{1,0:T(8,128)(2,1)}, bf16[1664,1024]{1,0:T(8,128)(2,1)}, u32[]{:S(2)}, u32[]{:S(2)}) collective-permute-start(bf16[1664,1024]{1,0:T(8,128)(2,1)} %fusion.refs_2_), channel_id=1, source_target_pairs={{0,8},{8,16},{16,24},{24,0},{1,9},{9,17},{17,25},{25,1},{2,10},{10... | collective-permute-start | bytes 10223624 | tf_op jit(solution)/shard_map/cond/branch_0_fun/ppermute | solution.py:257
  179.1 104.9 %collective-permute-start.7 = (bf16[640,1024]{1,0:T(8,128)(2,1)}, bf16[640,1024]{1,0:T(8,128)(2,1)}, u32[]{:S(2)}, u32[]{:S(2)}) collective-permute-start(bf16[640,1024]{1,0:T(8,128)(2,1)} %fusion.19.refs_2_), channel_id=1, source_target_pairs={{0,8},{8,16},{16,24},{24,0},{1,9},{9,17},{17,25},{25,1},{2,10},{10... | collective-permute-start | bytes 3932168 | tf_op jit(solution)/shard_map/cond/branch_0_fun/ppermute | solution.py:257
  179.1 122.1 %collective-permute-start.2 = (bf16[384,1024]{1,0:T(8,128)(2,1)}, bf16[384,1024]{1,0:T(8,128)(2,1)}, u32[]{:S(2)}, u32[]{:S(2)}) collective-permute-start(bf16[384,1024]{1,0:T(8,128)(2,1)} %fusion.22.refs_0_), channel_id=1, source_target_pairs={{0,8},{8,16},{16,24},{24,0},{1,9},{9,17},{17,25},{25,1},{2,10},{10... | collective-permute-start | bytes 2359304 | tf_op jit(solution)/shard_map/cond/branch_0_fun/ppermute | solution.py:257
  180.7 1.0 copy-start.10
  181.7 134.3 %collective-permute-start.3 = (bf16[384,1024]{1,0:T(8,128)(2,1)}, bf16[384,1024]{1,0:T(8,128)(2,1)S(1)}, u32[]{:S(2)}, u32[]{:S(2)}) collective-permute-start(bf16[384,1024]{1,0:T(8,128)(2,1)} %fusion.21.refs_2_), channel_id=1, source_target_pairs={{0,8},{8,16},{16,24},{24,0},{1,9},{9,17},{17,25},{25,1},{2,10},{10... | collective-permute-start | bytes 2359304 | tf_op jit(solution)/shard_map/cond/branch_0_fun/ppermute | solution.py:257
  316.0 0.9 copy-start.12
where the time goes:
time: 323 us; the launch traced here: 322 us
  Pallas kernels  151 us (47%)
  waiting for transfers between devices  101 us (31%)
  matrix products  49.6 us (15%)
  starting transfers between devices  11.6 us (4%)
  local copies, waits for them, and re-layouts  4.44 us (1%)
    ppermute x9, waiting for transfers between devices, send(): return lax.ppermute(value, 'rep', perm)  101 us
    pallas_call x1, Pallas kernels, scatter_call(): pl.pallas_call(partial(scatter_kernel, n), name='grad_scatter', out_shape...  71.6 us
    pallas_call x1, Pallas kernels, rest_call(): pl.pallas_call(partial(rest_kernel, n), name='rest_gather', out_shape=jax...  37.7 us
    dot_general x8, matrix products, halves(): lax.dot_general(shard_rows, delta, (((0,), (0,)), ((), ())), preferred_el...  28.9 us
    pallas_call x4, Pallas kernels, mix_call(): pl.pallas_call(partial(mix_kernel, first), name='mix', grid=(rows // tile...  25 us
    pallas_call x1, Pallas kernels, first_call(): pl.pallas_call(partial(first_kernel, n), name='first_gather', out_shape=(...  16.2 us
    ppermute x9, starting transfers between devices, send(): return lax.ppermute(value, 'rep', perm)  11.6 us
    dot_general x1, matrix products, exchange_at(): lax.dot_general(up_delta, up_point, contract_cols, preferred_element_type...  11.4 us
  transfers between devices with their start and end apart: 9, of which 3 were waited for; matrix products, arithmetic and copies ran while one was open for 14% of the time, Pallas kernels for 41%

commit v1 on v0

--- a/solution.py
+++ b/solution.py
@@ -11,7 +11,8 @@
 MESH = pl.DeviceIdType.MESH
 ANY = pl.BlockSpec(memory_space=pl.ANY)
 VMEM = pl.BlockSpec(memory_space=pltpu.VMEM)
-SPLITS = (3, 5, 13, 3)
+SPLITS = (3, 6, 13, 2)
+PIECES = 4
 
 
 def greet(me, n):
@@ -23,7 +24,7 @@
     pl.semaphore_wait(barrier, n - 1)
 
 
-def gather_body(n, tok, out, sems, between=None):
+def gather_body(n, tok, out, sems, between=None, later=None):
     send, recv, fsend, frecv, local = sems
     me = lax.axis_index("fsdp")
     rows = tok.shape[0]
@@ -61,6 +62,8 @@
         copy = remote(block(owner), owner, fsend.at[k], frecv.at[k], beside)
         copy.start()
         relays.append(copy)
+    if later is not None:
+        later()
     own.wait()
     near.wait_send()
     remote(tok, beside, send.at[0], recv.at[0], beside).wait_recv()
@@ -72,23 +75,75 @@
         remote(tok, owner, fsend.at[k], frecv.at[k], beside).wait_recv()
 
 
-def first_kernel(n, tok, gate, up, cot, out, gate_delta, up_delta, *sems):
-    rows = gate.shape[0]
-    tile = min(32, rows)
-
-    def deltas():
-        @pl.loop(0, rows // tile)
-        def _(i):
-            at = pl.ds(pl.multiple_of(i * tile, tile), tile)
-            g = gate[at, :].astype(jnp.float32)
-            u = up[at, :].astype(jnp.float32)
-            h = cot[at, :].astype(jnp.float32)
-            p = jax.nn.sigmoid(g)
-            hp = h * p
-            gate_delta[at, :] = (hp * u * (1.0 + g * (1.0 - p))).astype(jnp.bfloat16)
-            up_delta[at, :] = (hp * g).astype(jnp.bfloat16)
-
-    gather_body(n, tok, out, sems, deltas)
+def first_kernel(
+    n, factor, tokens, gate, up, cot, gate_num, up_num,
+    gate_delta, up_delta, gate_half, up_half,
+    land, turned, acts, grads, nums, load, store, *sems
+):
+    rows, first = gate.shape[0], gate_half.shape[0]
+    piece = rows // PIECES
+    tile = min(32, piece)
+    columns = min(256, gate.shape[1])
+    loads = []
+    for c in range(PIECES):
+        at = pl.ds(c * piece, piece)
+        for which, ref in enumerate((gate, up, cot)):
+            copy = pltpu.make_async_copy(ref.at[at, :], acts.at[which, at, :], load.at[which, c])
+            copy.start()
+            loads.append(copy)
+    num_loads = []
+    for which, ref in enumerate((gate_num, up_num)):
+        copy = pltpu.make_async_copy(
+            ref.at[pl.ds(0, first), :], nums.at[which], load.at[3, which]
+        )
+        copy.start()
+        num_loads.append(copy)
+
+    def deltas(pieces):
+        for c in pieces:
+            for copy in loads[3 * c : 3 * c + 3]:
+                copy.wait()
+
+            @pl.loop(0, piece // tile)
+            def _(i):
+                at = pl.ds(pl.multiple_of(c * piece + i * tile, tile), tile)
+                g = acts[0, at, :].astype(jnp.float32)
+                u = acts[1, at, :].astype(jnp.float32)
+                h = acts[2, at, :].astype(jnp.float32)
+                p = jax.nn.sigmoid(g)
+                hp = h * p
+                grads[0, at, :] = (hp * u * (1.0 + g * (1.0 - p))).astype(jnp.bfloat16)
+                grads[1, at, :] = (hp * g).astype(jnp.bfloat16)
+
+    half = PIECES // 2
+    gather_body(
+        n,
+        tokens.at[:, pl.ds(0, first)],
+        land,
+        sems,
+        lambda: deltas(range(half)),
+        lambda: deltas(range(half, PIECES)),
+    )
+    turned[...] = land[...].T
+    stores = []
+    for which, ref in enumerate((gate_delta, up_delta)):
+        copy = pltpu.make_async_copy(grads.at[which], ref, store.at[which])
+        copy.start()
+        stores.append(copy)
+    for which, out in enumerate((gate_half, up_half)):
+        num_loads[which].wait()
+
+        @pl.loop(0, gate.shape[1] // columns)
+        def _(j):
+            at = pl.ds(pl.multiple_of(j * columns, columns), columns)
+            total = jnp.dot(turned[...], grads[which, :, at], preferred_element_type=jnp.float32)
+            grad = (factor * total).astype(jnp.bfloat16)
+            out[:, at] = (
+                nums[which, :, at].astype(jnp.float32) - grad.astype(jnp.float32)
+            ).astype(jnp.bfloat16)
+
+    for copy in stores:
+        copy.wait()
 
 
 def rest_kernel(n, tok, after, out, *sems):
@@ -99,17 +154,28 @@
     return [pltpu.SemaphoreType.DMA((n // 2,))] * 4 + [pltpu.SemaphoreType.DMA((1,))]
 
 
-def first_call(n, tok, gate, up, cot):
-    like = jax.ShapeDtypeStruct(gate.shape, jnp.bfloat16)
+def first_call(n, first, factor, tokens, gate, up, cot, gate_num, up_num):
+    rows, cols = gate.shape
+    delta = jax.ShapeDtypeStruct((rows, cols), jnp.bfloat16)
+    half = jax.ShapeDtypeStruct((first, cols), jnp.bfloat16)
     return pl.pallas_call(
-        partial(first_kernel, n),
+        partial(first_kernel, n, factor),
         name="first_gather",
-        out_shape=(jax.ShapeDtypeStruct((n * tok.shape[0], tok.shape[1]), tok.dtype), like, like),
-        in_specs=[VMEM] * 4,
-        out_specs=(ANY, VMEM, VMEM),
-        scratch_shapes=gather_sems(n),
+        out_shape=(delta, delta, half, half),
+        in_specs=[ANY] * 6,
+        out_specs=(ANY, ANY, VMEM, VMEM),
+        scratch_shapes=[
+            pltpu.VMEM((rows, first), jnp.bfloat16),
+            pltpu.VMEM((first, rows), jnp.bfloat16),
+            pltpu.VMEM((3, rows, cols), jnp.bfloat16),
+            pltpu.VMEM((2, rows, cols), jnp.bfloat16),
+            pltpu.VMEM((2, first, cols), jnp.bfloat16),
+            pltpu.SemaphoreType.DMA((4, PIECES)),
+            pltpu.SemaphoreType.DMA((2,)),
+        ]
+        + gather_sems(n),
         compiler_params=pltpu.CompilerParams(collective_id=0, has_side_effects=True),
-    )(tok, gate, up, cot)
+    )(tokens, gate, up, cot, gate_num, up_num)
 
 
 def rest_call(n, ident, tok, after):
@@ -297,11 +363,9 @@
     depth = tokens.shape[1]
     factor = depth ** (-0.5)
     first = depth // sum(SPLITS) * SPLITS[0]
-    rows, gate_delta, up_delta = first_call(
-        n, tokens[:, :first], gate_saved, up_saved, hidden_grad
-    )
-    gate_first = halves(rows, gate_delta, gate_num[0, :first], factor)
-    up_first = halves(rows, up_delta, up_num[0, :first], factor)
+    gate_delta, up_delta, gate_first, up_first = first_call(
+        n, first, factor, tokens, gate_saved, up_saved, hidden_grad, gate_num[0], up_num[0]
+    )
     args = (
         tokens, gate_num[0], up_num[0], push_weight, gate_delta, up_delta, gate_first, up_first
     )

time: 323 us -> 313 us (0.969)
  matrix products: 49.6 us -> 39.5 us
    dot_general x8 -> x6, matrix products: 28.9 us -> 18.8 us  [halves(): lax.dot_general(shard_rows, delta, (((0,), (0,)), ((), ())), preferred_el...]
    ppermute x9, waiting for transfers between devices: 101 us -> 104 us  [send(): return lax.ppermute(value, 'rep', perm)]
  transfers between devices with their start and end apart: 9 -> 9, of which waited for: 3 -> 3; matrix products, arithmetic and copies ran while one was open for 14% -> 13% of each run, Pallas kernels for 41% -> 42%
where the time goes in v1:
time: 313 us; the launch traced here: 312 us
  Pallas kernels  149 us (48%)
  waiting for transfers between devices  104 us (33%)
  matrix products  39.5 us (13%)
  starting transfers between devices  11.8 us (4%)
    ppermute x9, waiting for transfers between devices, send(): return lax.ppermute(value, 'rep', perm)  104 us
    pallas_call x1, Pallas kernels, scatter_call(): pl.pallas_call(partial(scatter_kernel, n), name='grad_scatter', out_shape...  71.6 us
    pallas_call x1, Pallas kernels, rest_call(): pl.pallas_call(partial(rest_kernel, n), name='rest_gather', out_shape=jax...  37.9 us
    pallas_call x4, Pallas kernels, mix_call(): pl.pallas_call(partial(mix_kernel, first), name='mix', grid=(rows // tile...  24.4 us
    dot_general x6, matrix products, halves(): lax.dot_general(shard_rows, delta, (((0,), (0,)), ((), ())), preferred_el...  18.8 us
    pallas_call x1, Pallas kernels, first_call(): pl.pallas_call(partial(first_kernel, n, factor), name='first_gather', out...  15.6 us
    ppermute x9, starting transfers between devices, send(): return lax.ppermute(value, 'rep', perm)  11.8 us
    dot_general x1, matrix products, exchange_at(): lax.dot_general(up_delta, up_point, contract_cols, preferred_element_type...  11.4 us
  transfers between devices with their start and end apart: 9, of which 3 were waited for; matrix products, arithmetic and copies ran while one was open for 13% of the time, Pallas kernels for 42%

profile of v1, /device:TPU:0, one launch (start us, length us, event | category | flops | bytes accessed | tf_op | source)
XLA Modules:
  0.0 312.2 jit_solution(17571885744783855465)
XLA Ops:
  1.3 15.6 %first_gather.1 = (bf16[1024,1024]{1,0:T(8,128)(2,1)}, bf16[1024,1024]{1,0:T(8,128)(2,1)}, bf16[384,1024]{1,0:T(8,128)(2,1)S(1)}, bf16[384,1024]{1,0:T(8,128)(2,1)}) custom-call(bf16[128,3072]{1,0:T(8,128)(2,1)} %tokens.1, bf16[1024,1024]{1,0:T(8,128)(2,1)} %gate.1, bf16[1024,1024]{1,0:T(8,128)(2,1)} %up.1, bf16[1024,1024]{1,0:T(8,128)(2,1)} %cot.1, ...), custom_call_target="tpu_custom_call" | custom-call | tf_op jit(solution)/shard_map/first_gather/pallas_call | solution.py:161
  16.9 294.2 %conditional.1 = (bf16[128,3072]{1,0:T(8,128)(2,1)}, bf16[1,3072,1024]{2,1,0:T(8,128)(2,1)}, bf16[1,3072,1024]{2,1,0:T(8,128)(2,1)}, f32[1]{0:T(128)}) conditional(s32[]{:T(128)} %clamp.3, (bf16[384,1024]{1,0:T(8,128)(2,1)S(1)}, bf16[384,1024]{1,0:T(8,128)(2,1)}, bf16[3072,1024]{1,0:T(8,128)(2,1)}, bf16[1]{0:T(256)(128)(2,1)}, ...), branch_computations={%region_0.1_spmd, %region_1.2_spmd} | conditional | flops 24233115648 | bytes 582919680 | solution.py:373
  16.9 1.6 collective-permute-start
  18.6 1.6 collective-permute-start.1
  20.1 0.9 slice.41.tok
  21.0 37.9 %rest_gather.2 = bf16[1024,2688]{1,0:T(8,128)(2,1)} custom-call(bf16[128,2688]{1,0:T(8,128)(2,1)} %slice.41.tok, bf16[384,1024]{1,0:T(8,128)(2,1)S(1)} %get-tuple-element.32.refs_0_.after), custom_call_target="tpu_custom_call" | custom-call | bytes 100000000 | tf_op jit(solution)/shard_map/cond/branch_0_fun/rest_gather/pallas_call | solution.py:182
  59.0 0.0 slice-start.1
  59.0 4.6 %subtract_convert_fusion.3.refs_0_ = bf16[768,1024]{1,0:T(8,128)(2,1)S(1)} fusion(bf16[3072,1024]{1,0:T(8,128)(2,1)} %get-tuple-element.34, bf16[1024,1024]{1,0:T(8,128)(2,1)} %get-tuple-element.36, bf16[1024,2688]{1,0:T(8,128)(2,1)} %rest_gather.2), kind=kOutput, calls=%fused_computation.14 | convolution fusion | flops 1615331328 | bytes 6815744 | tf_op jit(solution)/shard_map/cond/branch_0_fun/dot_general | solution.py:299
  63.6 1.6 collective-permute-start.6
  65.2 0.3 copy-done.4
  65.6 5.4 %subtract_convert_fusion.1.refs_0_ = bf16[1664,1024]{1,0:T(8,128)(2,1)} fusion(bf16[3072,1024]{1,0:T(8,128)(2,1)S(1)} %bitcast.40, bf16[1024,1024]{1,0:T(8,128)(2,1)S(1)} %copy-done, bf16[1024,2688]{1,0:T(8,128)(2,1)S(1)} %copy-done.4), kind=kOutput, calls=%fused_computation.5 | convolution fusion | flops 3499884544 | bytes 12320768 | tf_op jit(solution)/shard_map/cond/branch_0_fun/dot_general | solution.py:299
  71.0 1.6 collective-permute-start.4
  72.5 0.2 collective-permute-start.8
  73.5 0.7 fusion.20.refs_0_
  74.2 0.0 slice-start.5
  74.2 9.2 %fusion = f32[3072,1024]{0,1:T(8,128)} fusion(bf16[1024,1024]{1,0:T(8,128)(2,1)S(1)} %copy-done, bf16[3072,1024]{1,0:T(8,128)(2,1)S(1)} %bitcast.40, f32[]{:T(128)} %bitcast), kind=kOutput, calls=%fused_computation.7 | convolution fusion | flops 6451888128 | bytes 20971524 | tf_op jit(solution)/shard_map/cond/branch_0_fun/dot_general | solution.py:344
  83.5 5.5 %subtract_convert_fusion.refs_2_ = bf16[1664,1024]{1,0:T(8,128)(2,1)} fusion(bf16[3072,1024]{1,0:T(8,128)(2,1)S(1)} %bitcast.47, bf16[1024,1024]{1,0:T(8,128)(2,1)S(1)} %copy-done.2, bf16[1024,2688]{1,0:T(8,128)(2,1)S(1)} %copy-done.4), kind=kOutput, calls=%fused_computation.3 | convolution fusion | flops 3499884544 | bytes 12320768 | tf_op jit(solution)/shard_map/cond/branch_0_fun/dot_general | solution.py:299
  88.9 1.9 subtract_convert_fusion.2.refs_2_
  90.9 84.4 %collective-permute-done.8 = bf16[1]{0:T(256)(128)(2,1)} collective-permute-done((bf16[1]{0:T(256)(128)(2,1)}, bf16[1]{0:T(256)(128)(2,1)}, u32[]{:S(2)}, u32[]{:S(2)}) %collective-permute-start.8) | collective-permute-done | bytes 34 | tf_op jit(solution)/shard_map/cond/branch_0_fun/ppermute | solution.py:323
  175.2 0.7 fusion.24.refs_2_
  176.0 0.3 collective-permute-start.7
  176.3 1.5 collective-permute-start.2
  177.8 1.2 copy-done.13
  179.0 3.4 %collective-permute-start.3 = (bf16[256,1024]{1,0:T(8,128)(2,1)S(1)}, bf16[256,1024]{1,0:T(8,128)(2,1)}, u32[]{:S(2)}, u32[]{:S(2)}) collective-permute-start(bf16[256,1024]{1,0:T(8,128)(2,1)S(1)} %fusion.24.refs_2_), channel_id=1, source_target_pairs={{0,8},{8,16},{16,24},{24,0},{1,9},{9,17},{17,25},{25,1},{2,10},{10... | collective-permute-start | bytes 1572872 | tf_op jit(solution)/shard_map/cond/branch_0_fun/ppermute | solution.py:323
  182.4 11.4 %fusion.2.term = bf16[1024,3072]{1,0:T(8,128)(2,1)} fusion(f32[3072,1024]{0,1:T(8,128)} %fusion, bf16[1024,1024]{1,0:T(8,128)(2,1)S(1)} %copy-done.2, bf16[3072,1024]{1,0:T(8,128)(2,1)S(1)} %bitcast.47, f32[]{:T(128)} %bitcast), kind=kOutput, calls=%fused_computation.9 | convolution fusion | flops 6461325312 | bytes 27262980 | tf_op jit(solution)/shard_map/cond/branch_0_fun/dot_general | solution.py:345
  193.8 71.6 %grad_scatter.2.refs_4_ = bf16[128,3072]{1,0:T(8,128)(2,1)} custom-call(bf16[1024,3072]{1,0:T(8,128)(2,1)} %fusion.2.term), custom_call_target="tpu_custom_call" | custom-call | bytes 200000000 | tf_op jit(solution)/shard_map/cond/branch_0_fun/grad_scatter/pallas_call | solution.py:233
  266.7 4.3 %mix.8 = (bf16[3072,1024]{1,0:T(8,128)(2,1)}, bf16[3072,1024]{1,0:T(8,128)(2,1)}, bf16[128,3072]{1,0:T(8,128)(2,1)}) custom-call(bf16[384,1024]{1,0:T(8,128)(2,1)S(1)} %get-tuple-element.32.refs_0_.after, bf16[384,1024]{1,0:T(8,128)(2,1)} %collective-permute-done.refs_1_, bf16[384,1024]{1,0:T(8,128)(2,1)} %get-tuple-element.33.refs_2_, ...), custom_call_target="tpu_custom_call" | custom-call | flops 1572864 | bytes 4718592 | tf_op jit(solution)/shard_map/cond/branch_0_fun/mix/pallas_call | solution.py:284
  271.0 16.7 %collective-permute-done.7.refs_3_ = bf16[768,1024]{1,0:T(8,128)(2,1)} collective-permute-done((bf16[768,1024]{1,0:T(8,128)(2,1)S(1)}, bf16[768,1024]{1,0:T(8,128)(2,1)}, u32[]{:S(2)}, u32[]{:S(2)}) %collective-permute-start.7) | collective-permute-done | bytes 1572896 | tf_op jit(solution)/shard_map/cond/branch_0_fun/ppermute | solution.py:323
  287.7 5.9 %mix.9 = (bf16[3072,1024]{1,0:T(8,128)(2,1)}, bf16[3072,1024]{1,0:T(8,128)(2,1)}) custom-call(bf16[768,1024]{1,0:T(8,128)(2,1)} %copy-done.11, bf16[768,1024]{1,0:T(8,128)(2,1)} %copy-done.13, bf16[768,1024]{1,0:T(8,128)(2,1)} %copy-done.15, bf16[768,1024]{1,0:T(8,128)(2,1)} %collective-permute-done.7.refs_3_, ...), custom_call_target="tpu_custom_call", output_to_operand_aliasing={{0}: (5, {}), {1}: (6, {})} | custom-call | flops 3145728 | bytes 9437184 | tf_op jit(solution)/shard_map/cond/branch_0_fun/mix/pallas_call | solution.py:284
  293.6 11.8 %mix.10 = (bf16[3072,1024]{1,0:T(8,128)(2,1)}, bf16[3072,1024]{1,0:T(8,128)(2,1)}) custom-call(bf16[1664,1024]{1,0:T(8,128)(2,1)} %subtract_convert_fusion.1.refs_0_, bf16[1664,1024]{1,0:T(8,128)(2,1)} %collective-permute-done.4.refs_1_, bf16[1664,1024]{1,0:T(8,128)(2,1)} %subtract_convert_fusion.refs_2_, ...), custom_call_target="tpu_custom_call", output_to_operand_aliasing={{0}: (5, {}), {1}: (6, {})} | custom-call | flops 6815744 | bytes 20447232 | tf_op jit(solution)/shard_map/cond/branch_0_fun/mix/pallas_call | solution.py:284
  305.4 3.3 %collective-permute-done.3.refs_3_ = bf16[256,1024]{1,0:T(8,128)(2,1)} collective-permute-done((bf16[256,1024]{1,0:T(8,128)(2,1)S(1)}, bf16[256,1024]{1,0:T(8,128)(2,1)}, u32[]{:S(2)}, u32[]{:S(2)}) %collective-permute-start.3) | collective-permute-done | bytes 524320 | tf_op jit(solution)/shard_map/cond/branch_0_fun/ppermute | solution.py:323
  308.7 2.4 mix.11
  (31 shorter events, 0.1 us)
Async XLA Ops:
  1.3 15.6 %copy-start.6 = (bf16[128,3072]{1,0:T(8,128)(2,1)S(1)}, bf16[128,3072]{1,0:T(8,128)(2,1)}, u32[]{:S(2)}) copy-start(bf16[128,3072]{1,0:T(8,128)(2,1)} %tokens.1) | copy-start | bytes 2359300
  16.9 159.1 %collective-permute-start = (bf16[384,1024]{1,0:T(8,128)(2,1)S(1)}, bf16[384,1024]{1,0:T(8,128)(2,1)}, u32[]{:S(2)}, u32[]{:S(2)}) collective-permute-start(bf16[384,1024]{1,0:T(8,128)(2,1)S(1)} %get-tuple-element.32.refs_0_.after), channel_id=1, source_target_pairs={{0,8},{8,16},{16,24},{24,0},{1,9},{9,17},{17,25},{25,1},{2,10},{10... | collective-permute-start | bytes 2359304 | tf_op jit(solution)/shard_map/cond/branch_0_fun/ppermute | solution.py:323
  18.6 157.8 %collective-permute-start.1 = (bf16[384,1024]{1,0:T(8,128)(2,1)}, bf16[384,1024]{1,0:T(8,128)(2,1)}, u32[]{:S(2)}, u32[]{:S(2)}) collective-permute-start(bf16[384,1024]{1,0:T(8,128)(2,1)} %get-tuple-element.33.refs_2_), channel_id=1, source_target_pairs={{0,8},{8,16},{16,24},{24,0},{1,9},{9,17},{17,25},{25,1},{2,10},{10... | collective-permute-start | bytes 2359304 | tf_op jit(solution)/shard_map/cond/branch_0_fun/ppermute | solution.py:323
  21.0 44.2 %slice-start = ((s8[6291456]{0:T(1024)(128)(4,1)}), s8[2097152]{0:T(1024)(128)(4,1)S(1)}, s32[]{:S(2)}) async-start(s8[6291456]{0:T(1024)(128)(4,1)} %bitcast.39), calls=%async_computation | async-start | bytes 4194304 | tf_op jit(solution)/shard_map/cond
  59.0 6.3 %slice-start.1 = ((s8[6291456]{0:T(1024)(128)(4,1)}), s8[4194304]{0:T(1024)(128)(4,1)S(1)}, s32[]{:S(2)}) async-start(s8[6291456]{0:T(1024)(128)(4,1)} %bitcast.39), calls=%async_computation.1 | async-start | bytes 8388608 | tf_op jit(solution)/shard_map/cond
  59.0 6.2 %copy-start = (bf16[1024,1024]{1,0:T(8,128)(2,1)S(1)}, bf16[1024,1024]{1,0:T(8,128)(2,1)}, u32[]{:S(2)}) copy-start(bf16[1024,1024]{1,0:T(8,128)(2,1)} %get-tuple-element.36) | copy-start | bytes 6291460 | tf_op jit(solution)/shard_map/cond
  59.0 6.6 %copy-start.4 = (bf16[1024,2688]{1,0:T(8,128)(2,1)S(1)}, bf16[1024,2688]{1,0:T(8,128)(2,1)}, u32[]{:S(2)}) copy-start(bf16[1024,2688]{1,0:T(8,128)(2,1)} %rest_gather.2) | copy-start | bytes 16515076 | tf_op jit(solution)/shard_map/cond
  63.6 7.4 %copy-start.11 = (bf16[768,1024]{1,0:T(8,128)(2,1)}, bf16[768,1024]{1,0:T(8,128)(2,1)S(1)}, u32[]{:S(2)}) copy-start(bf16[768,1024]{1,0:T(8,128)(2,1)S(1)} %subtract_convert_fusion.3.refs_0_) | copy-start | bytes 4718596 | tf_op jit(solution)/shard_map/cond
  63.6 114.2 %collective-permute-start.6 = (bf16[768,1024]{1,0:T(8,128)(2,1)S(1)}, bf16[768,1024]{1,0:T(8,128)(2,1)S(1)}, u32[]{:S(2)}, u32[]{:S(2)}) collective-permute-start(bf16[768,1024]{1,0:T(8,128)(2,1)S(1)} %subtract_convert_fusion.3.refs_0_), channel_id=1, source_target_pairs={{0,8},{8,16},{16,24},{24,0},{1,9},{9,17},{17,25},{25,1},{2,10},{10... | collective-permute-start | bytes 4718600 | tf_op jit(solution)/shard_map/cond/branch_0_fun/ppermute | solution.py:323
  71.0 222.6 %collective-permute-start.4 = (bf16[1664,1024]{1,0:T(8,128)(2,1)}, bf16[1664,1024]{1,0:T(8,128)(2,1)}, u32[]{:S(2)}, u32[]{:S(2)}) collective-permute-start(bf16[1664,1024]{1,0:T(8,128)(2,1)} %subtract_convert_fusion.1.refs_0_), channel_id=1, source_target_pairs={{0,8},{8,16},{16,24},{24,0},{1,9},{9,17},{17,25},{25,1},{2,10},{10... | collective-permute-start | bytes 10223624 | tf_op jit(solution)/shard_map/cond/branch_0_fun/ppermute | solution.py:323
  72.5 102.7 %collective-permute-start.8 = (bf16[1]{0:T(256)(128)(2,1)}, bf16[1]{0:T(256)(128)(2,1)}, u32[]{:S(2)}, u32[]{:S(2)}) collective-permute-start(bf16[1]{0:T(256)(128)(2,1)} %get-tuple-element.35), channel_id=1, source_target_pairs={{0,8},{8,16},{16,24},{24,0},{1,9},{9,17},{17,25},{25,1},{2,10},{10... | collective-permute-start | bytes 14 | tf_op jit(solution)/shard_map/cond/branch_0_fun/ppermute | solution.py:323
  73.5 10.0 %slice-start.4 = ((s8[6291456]{0:T(1024)(128)(4,1)}), s8[4194304]{0:T(1024)(128)(4,1)S(1)}, s32[]{:S(2)}) async-start(s8[6291456]{0:T(1024)(128)(4,1)} %bitcast.46), calls=%async_computation.4 | async-start | bytes 8388608 | tf_op jit(solution)/shard_map/cond
  74.2 102.1 %copy-start.7 = (bf16[256,1024]{1,0:T(8,128)(2,1)}, bf16[256,1024]{1,0:T(8,128)(2,1)S(1)}, u32[]{:S(2)}) copy-start(bf16[256,1024]{1,0:T(8,128)(2,1)S(1)} %fusion.20.refs_0_) | copy-start | bytes 1572868 | tf_op jit(solution)/shard_map/cond
  74.2 9.3 %slice-start.5 = ((s8[6291456]{0:T(1024)(128)(4,1)}), s8[2097152]{0:T(1024)(128)(4,1)S(1)}, s32[]{:S(2)}) async-start(s8[6291456]{0:T(1024)(128)(4,1)} %bitcast.46), calls=%async_computation.5 | async-start | bytes 4194304 | tf_op jit(solution)/shard_map/cond
  74.2 9.2 %copy-start.2 = (bf16[1024,1024]{1,0:T(8,128)(2,1)S(1)}, bf16[1024,1024]{1,0:T(8,128)(2,1)}, u32[]{:S(2)}) copy-start(bf16[1024,1024]{1,0:T(8,128)(2,1)} %get-tuple-element.38) | copy-start | bytes 6291460 | tf_op jit(solution)/shard_map/cond
  90.9 102.9 %copy-start.15 = (bf16[768,1024]{1,0:T(8,128)(2,1)}, bf16[768,1024]{1,0:T(8,128)(2,1)S(1)}, u32[]{:S(2)}) copy-start(bf16[768,1024]{1,0:T(8,128)(2,1)S(1)} %subtract_convert_fusion.2.refs_2_) | copy-start | bytes 4718596 | tf_op jit(solution)/shard_map/cond
  175.2 118.3 %collective-permute-start.5 = (bf16[1664,1024]{1,0:T(8,128)(2,1)}, bf16[1664,1024]{1,0:T(8,128)(2,1)}, u32[]{:S(2)}, u32[]{:S(2)}) collective-permute-start(bf16[1664,1024]{1,0:T(8,128)(2,1)} %subtract_convert_fusion.refs_2_), channel_id=1, source_target_pairs={{0,8},{8,16},{16,24},{24,0},{1,9},{9,17},{17,25},{25,1},{2,10},{10... | collective-permute-start | bytes 10223624 | tf_op jit(solution)/shard_map/cond/branch_0_fun/ppermute | solution.py:323
  176.0 17.8 %copy-start.9 = (bf16[256,1024]{1,0:T(8,128)(2,1)}, bf16[256,1024]{1,0:T(8,128)(2,1)S(1)}, u32[]{:S(2)}) copy-start(bf16[256,1024]{1,0:T(8,128)(2,1)S(1)} %fusion.24.refs_2_) | copy-start | bytes 1572868 | tf_op jit(solution)/shard_map/cond
  176.0 111.6 %collective-permute-start.7 = (bf16[768,1024]{1,0:T(8,128)(2,1)S(1)}, bf16[768,1024]{1,0:T(8,128)(2,1)}, u32[]{:S(2)}, u32[]{:S(2)}) collective-permute-start(bf16[768,1024]{1,0:T(8,128)(2,1)S(1)} %subtract_convert_fusion.2.refs_2_), channel_id=1, source_target_pairs={{0,8},{8,16},{16,24},{24,0},{1,9},{9,17},{17,25},{25,1},{2,10},{10... | collective-permute-start | bytes 4718600 | tf_op jit(solution)/shard_map/cond/branch_0_fun/ppermute | solution.py:323
  176.3 129.0 %collective-permute-start.2 = (bf16[256,1024]{1,0:T(8,128)(2,1)S(1)}, bf16[256,1024]{1,0:T(8,128)(2,1)}, u32[]{:S(2)}, u32[]{:S(2)}) collective-permute-start(bf16[256,1024]{1,0:T(8,128)(2,1)S(1)} %fusion.20.refs_0_), channel_id=1, source_target_pairs={{0,8},{8,16},{16,24},{24,0},{1,9},{9,17},{17,25},{25,1},{2,10},{10... | collective-permute-start | bytes 1572872 | tf_op jit(solution)/shard_map/cond/branch_0_fun/ppermute | solution.py:323
  177.8 1.2 copy-start.13
  179.0 129.7 %collective-permute-start.3 = (bf16[256,1024]{1,0:T(8,128)(2,1)S(1)}, bf16[256,1024]{1,0:T(8,128)(2,1)}, u32[]{:S(2)}, u32[]{:S(2)}) collective-permute-start(bf16[256,1024]{1,0:T(8,128)(2,1)S(1)} %fusion.24.refs_2_), channel_id=1, source_target_pairs={{0,8},{8,16},{16,24},{24,0},{1,9},{9,17},{17,25},{25,1},{2,10},{10... | collective-permute-start | bytes 1572872 | tf_op jit(solution)/shard_map/cond/branch_0_fun/ppermute | solution.py:323

commit v2 on v1

--- a/solution.py
+++ b/solution.py
@@ -11,7 +11,7 @@
 MESH = pl.DeviceIdType.MESH
 ANY = pl.BlockSpec(memory_space=pl.ANY)
 VMEM = pl.BlockSpec(memory_space=pltpu.VMEM)
-SPLITS = (3, 6, 13, 2)
+SPLITS = (3, 5, 14, 2)
 PIECES = 4
 
 
@@ -324,9 +324,12 @@
 
     own = [(gate_first, up_first)]
     got = [(send(gate_first), send(up_first))]
-    rest = rest_call(n, 1 + 2 * exponent, tokens[:, bounds[1] :], gate_first)
     for low, high in zip(bounds[1:-1], bounds[2:]):
-        rows = rest[:, low - bounds[1] : high - bounds[1]]
+        if len(got) == 1:
+            start, rest = low, rest_call(n, 1 + 3 * exponent, tokens[:, low:high], up_first)
+        elif len(got) == 2:
+            start, rest = low, rest_call(n, 2 + 3 * exponent, tokens[:, low:], own[-1][1])
+        rows = rest[:, low - start : high - start]
         own.append(
             (
                 halves(rows, gate_delta, gate_num[low:high], factor),
@@ -344,7 +347,7 @@
         lax.dot_general(gate_delta, gate_point, contract_cols, preferred_element_type=jnp.float32)
         + lax.dot_general(up_delta, up_point, contract_cols, preferred_element_type=jnp.float32)
     )
-    input_grad = scatter_call(n, 2 + 2 * exponent, term.astype(jnp.bfloat16))
+    input_grad = scatter_call(n, 3 + 3 * exponent, term.astype(jnp.bfloat16))
     mixed = None
     for at, low in enumerate(bounds[:-1]):
         parts = (own[at][0], got[at][0], own[at][1], got[at][1])

time: 313 us -> 304 us (0.971)
  waiting for transfers between devices: 104 us -> 83.4 us
  Pallas kernels: 149 us -> 155 us
  matrix products: 39.5 us -> 45 us
    ppermute x9, waiting for transfers between devices: 104 us -> 83.4 us  [send(): return lax.ppermute(value, 'rep', perm)]
    pallas_call x1 -> x2, Pallas kernels: 37.9 us -> 43.9 us  [rest_call(): pl.pallas_call(partial(rest_kernel, n), name='rest_gather', out_shape=jax...]
    dot_general x6, matrix products: 18.8 us -> 24.3 us  [halves(): lax.dot_general(shard_rows, delta, (((0,), (0,)), ((), ())), preferred_el...]
  transfers between devices with their start and end apart: 9 -> 9, of which waited for: 3 -> 3; matrix products, arithmetic and copies ran while one was open for 13% -> 16% of each run, Pallas kernels for 42% -> 45%
where the time goes in v2:
time: 304 us; the launch traced here: 303 us
  Pallas kernels  155 us (51%)
  waiting for transfers between devices  83.4 us (27%)
  matrix products  45 us (15%)
  starting transfers between devices  11.6 us (4%)
  local copies, waits for them, and re-layouts  3.06 us (1%)
    ppermute x9, waiting for transfers between devices, send(): return lax.ppermute(value, 'rep', perm)  83.4 us
    pallas_call x1, Pallas kernels, scatter_call(): pl.pallas_call(partial(scatter_kernel, n), name='grad_scatter', out_shape...  71.7 us
    pallas_call x2, Pallas kernels, rest_call(): pl.pallas_call(partial(rest_kernel, n), name='rest_gather', out_shape=jax...  43.9 us
    dot_general x6, matrix products, halves(): lax.dot_general(shard_rows, delta, (((0,), (0,)), ((), ())), preferred_el...  24.3 us
    pallas_call x4, Pallas kernels, mix_call(): pl.pallas_call(partial(mix_kernel, first), name='mix', grid=(rows // tile...  24.2 us
    pallas_call x1, Pallas kernels, first_call(): pl.pallas_call(partial(first_kernel, n, factor), name='first_gather', out...  15.7 us
    ppermute x9, starting transfers between devices, send(): return lax.ppermute(value, 'rep', perm)  11.6 us
    dot_general x1, matrix products, exchange_at(): lax.dot_general(up_delta, up_point, contract_cols, preferred_element_type...  11.4 us
  transfers between devices with their start and end apart: 9, of which 3 were waited for; matrix products, arithmetic and copies ran while one was open for 16% of the time, Pallas kernels for 45%

profile of v2, /device:TPU:0, one launch (start us, length us, event | category | flops | bytes accessed | tf_op | source)
XLA Modules:
  0.0 303.2 jit_solution(14620942443882053227)
XLA Ops:
  1.3 15.7 %first_gather.1 = (bf16[1024,1024]{1,0:T(8,128)(2,1)}, bf16[1024,1024]{1,0:T(8,128)(2,1)S(1)}, bf16[384,1024]{1,0:T(8,128)(2,1)}, bf16[384,1024]{1,0:T(8,128)(2,1)S(1)}) custom-call(bf16[128,3072]{1,0:T(8,128)(2,1)} %tokens.1, bf16[1024,1024]{1,0:T(8,128)(2,1)} %gate.1, bf16[1024,1024]{1,0:T(8,128)(2,1)} %up.1, bf16[1024,1024]{1,0:T(8,128)(2,1)} %cot.1, ...), custom_call_target="tpu_custom_call" | custom-call | tf_op jit(solution)/shard_map/first_gather/pallas_call | solution.py:161
  17.0 285.1 %conditional.1 = (bf16[128,3072]{1,0:T(8,128)(2,1)}, bf16[1,3072,1024]{2,1,0:T(8,128)(2,1)}, bf16[1,3072,1024]{2,1,0:T(8,128)(2,1)}, f32[1]{0:T(128)}) conditional(s32[]{:T(128)} %clamp.3, (bf16[384,1024]{1,0:T(8,128)(2,1)}, bf16[384,1024]{1,0:T(8,128)(2,1)S(1)}, bf16[3072,1024]{1,0:T(8,128)(2,1)}, bf16[1]{0:T(256)(128)(2,1)}, ...), branch_computations={%region_0.1_spmd, %region_1.2_spmd} | conditional | flops 24233115648 | bytes 680822272 | solution.py:376
  17.0 1.6 collective-permute-start.1
  18.7 1.6 collective-permute-start
  20.2 1.6 slice.43.tok
  21.8 13.6 %rest_gather.4 = bf16[1024,640]{1,0:T(8,128)(2,1)} custom-call(bf16[128,640]{1,0:T(8,128)(2,1)} %slice.43.tok, bf16[384,1024]{1,0:T(8,128)(2,1)S(1)} %get-tuple-element.33.refs_2_.after), custom_call_target="tpu_custom_call" | custom-call | bytes 100000000 | tf_op jit(solution)/shard_map/cond/branch_0_fun/rest_gather/pallas_call | solution.py:182
  35.5 4.4 %subtract_convert_fusion.3.after.refs_2_ = bf16[640,1024]{1,0:T(8,128)(2,1)} fusion(bf16[3072,1024]{1,0:T(8,128)(2,1)} %get-tuple-element.37, bf16[1024,640]{1,0:T(8,128)(2,1)} %rest_gather.4, bf16[1024,1024]{1,0:T(8,128)(2,1)S(1)} %get-tuple-element.38), kind=kOutput, calls=%fused_computation.16 | convolution fusion | flops 1346109440 | bytes 6029312 | tf_op jit(solution)/shard_map/cond/branch_0_fun/dot_general | solution.py:299
  39.9 1.6 collective-permute-start.7
  41.5 0.8 slice.41.tok
  42.4 30.2 %rest_gather.5 = bf16[1024,2048]{1,0:T(8,128)(2,1)} custom-call(bf16[128,2048]{1,0:T(8,128)(2,1)} %slice.41.tok, bf16[640,1024]{1,0:T(8,128)(2,1)} %subtract_convert_fusion.3.after.refs_2_), custom_call_target="tpu_custom_call" | custom-call | bytes 100000000 | tf_op jit(solution)/shard_map/cond/branch_0_fun/rest_gather/pallas_call | solution.py:182
  72.6 9.9 %subtract_convert_fusion.1.refs_0_ = bf16[1792,1024]{1,0:T(8,128)(2,1)} fusion(bf16[3072,1024]{1,0:T(8,128)(2,1)} %get-tuple-element.34, bf16[1024,1024]{1,0:T(8,128)(2,1)} %get-tuple-element.36, bf16[1024,2048]{1,0:T(8,128)(2,1)} %rest_gather.5), kind=kOutput, calls=%fused_computation.5 | convolution fusion | flops 3769106432 | bytes 13107200 | tf_op jit(solution)/shard_map/cond/branch_0_fun/dot_general | solution.py:299
  82.5 0.2 collective-permute-start.4
  82.7 1.6 collective-permute-start.8
  85.0 0.0 slice-start.5
  85.1 9.3 %fusion = f32[3072,1024]{0,1:T(8,128)} fusion(bf16[1024,1024]{1,0:T(8,128)(2,1)S(1)} %copy-done, bf16[3072,1024]{1,0:T(8,128)(2,1)S(1)} %bitcast.44, f32[]{:T(128)} %bitcast), kind=kOutput, calls=%fused_computation.7 | convolution fusion | flops 6451888128 | bytes 20971524 | tf_op jit(solution)/shard_map/cond/branch_0_fun/dot_general | solution.py:347
  94.3 5.8 %subtract_convert_fusion.refs_2_ = bf16[1792,1024]{1,0:T(8,128)(2,1)} fusion(bf16[3072,1024]{1,0:T(8,128)(2,1)S(1)} %bitcast.51, bf16[1024,1024]{1,0:T(8,128)(2,1)S(1)} %copy-done.3, bf16[1024,2048]{1,0:T(8,128)(2,1)S(1)} %copy-done.6), kind=kOutput, calls=%fused_computation.3 | convolution fusion | flops 3769106432 | bytes 13107200 | tf_op jit(solution)/shard_map/cond/branch_0_fun/dot_general | solution.py:299
  100.2 0.7 fusion.14.refs_0_
  100.9 0.6 copy-done.16
  101.5 2.6 subtract_convert_fusion.2.refs_0_
  104.1 62.2 %collective-permute-done.8 = bf16[1]{0:T(256)(128)(2,1)} collective-permute-done((bf16[1]{0:T(256)(128)(2,1)}, bf16[1]{0:T(256)(128)(2,1)}, u32[]{:S(2)}, u32[]{:S(2)}) %collective-permute-start.8) | collective-permute-done | bytes 34 | tf_op jit(solution)/shard_map/cond/branch_0_fun/ppermute | solution.py:323
  166.3 0.7 fusion.18.refs_2_
  167.1 0.1 collective-permute-start.6
  167.2 1.5 collective-permute-start.2
  168.7 3.4 %collective-permute-start.3 = (bf16[256,1024]{1,0:T(8,128)(2,1)S(1)}, bf16[256,1024]{1,0:T(8,128)(2,1)}, u32[]{:S(2)}, u32[]{:S(2)}) collective-permute-start(bf16[256,1024]{1,0:T(8,128)(2,1)S(1)} %fusion.18.refs_2_), channel_id=1, source_target_pairs={{0,8},{8,16},{16,24},{24,0},{1,9},{9,17},{17,25},{25,1},{2,10},{10... | collective-permute-start | bytes 1572872 | tf_op jit(solution)/shard_map/cond/branch_0_fun/ppermute | solution.py:323
  172.1 11.4 %fusion.2.term = bf16[1024,3072]{1,0:T(8,128)(2,1)} fusion(f32[3072,1024]{0,1:T(8,128)} %fusion, bf16[1024,1024]{1,0:T(8,128)(2,1)S(1)} %copy-done.3, bf16[3072,1024]{1,0:T(8,128)(2,1)S(1)} %bitcast.51, f32[]{:T(128)} %bitcast), kind=kOutput, calls=%fused_computation.9 | convolution fusion | flops 6461325312 | bytes 27262980 | tf_op jit(solution)/shard_map/cond/branch_0_fun/dot_general | solution.py:348
  183.5 71.7 %grad_scatter.2.refs_4_ = bf16[128,3072]{1,0:T(8,128)(2,1)} custom-call(bf16[1024,3072]{1,0:T(8,128)(2,1)} %fusion.2.term), custom_call_target="tpu_custom_call" | custom-call | bytes 200000000 | tf_op jit(solution)/shard_map/cond/branch_0_fun/grad_scatter/pallas_call | solution.py:233
  256.6 4.0 %mix.8 = (bf16[3072,1024]{1,0:T(8,128)(2,1)}, bf16[3072,1024]{1,0:T(8,128)(2,1)}, bf16[128,3072]{1,0:T(8,128)(2,1)}) custom-call(bf16[384,1024]{1,0:T(8,128)(2,1)S(1)} %copy-done.10, bf16[384,1024]{1,0:T(8,128)(2,1)} %collective-permute-done.refs_1_, bf16[384,1024]{1,0:T(8,128)(2,1)S(1)} %get-tuple-element.33.refs_2_.after, ...), custom_call_target="tpu_custom_call" | custom-call | flops 1572864 | bytes 4718592 | tf_op jit(solution)/shard_map/cond/branch_0_fun/mix/pallas_call | solution.py:284
  260.5 18.2 %collective-permute-done.6.refs_1_ = bf16[640,1024]{1,0:T(8,128)(2,1)} collective-permute-done((bf16[640,1024]{1,0:T(8,128)(2,1)}, bf16[640,1024]{1,0:T(8,128)(2,1)}, u32[]{:S(2)}, u32[]{:S(2)}) %collective-permute-start.6) | collective-permute-done | bytes 1310752 | tf_op jit(solution)/shard_map/cond/branch_0_fun/ppermute | solution.py:323
  278.7 5.4 %mix.9 = (bf16[3072,1024]{1,0:T(8,128)(2,1)}, bf16[3072,1024]{1,0:T(8,128)(2,1)}) custom-call(bf16[640,1024]{1,0:T(8,128)(2,1)} %subtract_convert_fusion.2.refs_0_, bf16[640,1024]{1,0:T(8,128)(2,1)} %collective-permute-done.6.refs_1_, bf16[640,1024]{1,0:T(8,128)(2,1)} %subtract_convert_fusion.3.after.refs_2_, ...), custom_call_target="tpu_custom_call", output_to_operand_aliasing={{0}: (5, {}), {1}: (6, {})} | custom-call | flops 2621440 | bytes 7864320 | tf_op jit(solution)/shard_map/cond/branch_0_fun/mix/pallas_call | solution.py:284
  284.2 12.4 %mix.10 = (bf16[3072,1024]{1,0:T(8,128)(2,1)}, bf16[3072,1024]{1,0:T(8,128)(2,1)}) custom-call(bf16[1792,1024]{1,0:T(8,128)(2,1)} %subtract_convert_fusion.1.refs_0_, bf16[1792,1024]{1,0:T(8,128)(2,1)} %collective-permute-done.4.refs_1_, bf16[1792,1024]{1,0:T(8,128)(2,1)} %subtract_convert_fusion.refs_2_, ...), custom_call_target="tpu_custom_call", output_to_operand_aliasing={{0}: (5, {}), {1}: (6, {})} | custom-call | flops 7340032 | bytes 22020096 | tf_op jit(solution)/shard_map/cond/branch_0_fun/mix/pallas_call | solution.py:284
  296.6 3.1 %collective-permute-done.3.refs_3_ = bf16[256,1024]{1,0:T(8,128)(2,1)} collective-permute-done((bf16[256,1024]{1,0:T(8,128)(2,1)S(1)}, bf16[256,1024]{1,0:T(8,128)(2,1)}, u32[]{:S(2)}, u32[]{:S(2)}) %collective-permute-start.3) | collective-permute-done | bytes 524320 | tf_op jit(solution)/shard_map/cond/branch_0_fun/ppermute | solution.py:323
  299.7 2.4 mix.11
  (35 shorter events, 0.1 us)
Async XLA Ops:
  17.0 22.9 %copy-start.2 = (bf16[1024,1024]{1,0:T(8,128)(2,1)}, bf16[1024,1024]{1,0:T(8,128)(2,1)S(1)}, u32[]{:S(2)}) copy-start(bf16[1024,1024]{1,0:T(8,128)(2,1)S(1)} %get-tuple-element.38) | copy-start | bytes 6291460 | tf_op jit(solution)/shard_map/cond
  17.0 150.0 %collective-permute-start.1 = (bf16[384,1024]{1,0:T(8,128)(2,1)S(1)}, bf16[384,1024]{1,0:T(8,128)(2,1)}, u32[]{:S(2)}, u32[]{:S(2)}) collective-permute-start(bf16[384,1024]{1,0:T(8,128)(2,1)S(1)} %get-tuple-element.33.refs_2_.after), channel_id=1, source_target_pairs={{0,8},{8,16},{16,24},{24,0},{1,9},{9,17},{17,25},{25,1},{2,10},{10... | collective-permute-start | bytes 2359304 | tf_op jit(solution)/shard_map/cond/branch_0_fun/ppermute | solution.py:323
  18.7 148.5 %collective-permute-start = (bf16[384,1024]{1,0:T(8,128)(2,1)}, bf16[384,1024]{1,0:T(8,128)(2,1)}, u32[]{:S(2)}, u32[]{:S(2)}) collective-permute-start(bf16[384,1024]{1,0:T(8,128)(2,1)} %get-tuple-element.32.refs_0_), channel_id=1, source_target_pairs={{0,8},{8,16},{16,24},{24,0},{1,9},{9,17},{17,25},{25,1},{2,10},{10... | collective-permute-start | bytes 2359304 | tf_op jit(solution)/shard_map/cond/branch_0_fun/ppermute | solution.py:323
  35.5 6.0 %copy-start.8 = (bf16[128,3072]{1,0:T(8,128)(2,1)S(1)}, bf16[128,3072]{1,0:T(8,128)(2,1)}, u32[]{:S(2)}) copy-start(bf16[128,3072]{1,0:T(8,128)(2,1)} %get-tuple-element.40) | copy-start | bytes 2359300 | tf_op jit(solution)/shard_map/cond
  39.9 128.8 %collective-permute-start.7 = (bf16[640,1024]{1,0:T(8,128)(2,1)}, bf16[640,1024]{1,0:T(8,128)(2,1)}, u32[]{:S(2)}, u32[]{:S(2)}) collective-permute-start(bf16[640,1024]{1,0:T(8,128)(2,1)} %subtract_convert_fusion.3.after.refs_2_), channel_id=1, source_target_pairs={{0,8},{8,16},{16,24},{24,0},{1,9},{9,17},{17,25},{25,1},{2,10},{10... | collective-permute-start | bytes 3932168 | tf_op jit(solution)/shard_map/cond/branch_0_fun/ppermute | solution.py:323
  42.4 42.6 %slice-start = ((s8[6291456]{0:T(1024)(128)(4,1)}), s8[2097152]{0:T(1024)(128)(4,1)S(1)}, s32[]{:S(2)}) async-start(s8[6291456]{0:T(1024)(128)(4,1)} %bitcast.43), calls=%async_computation | async-start | bytes 4194304 | tf_op jit(solution)/shard_map/cond
  72.6 12.4 %slice-start.1 = ((s8[6291456]{0:T(1024)(128)(4,1)}), s8[4194304]{0:T(1024)(128)(4,1)S(1)}, s32[]{:S(2)}) async-start(s8[6291456]{0:T(1024)(128)(4,1)} %bitcast.43), calls=%async_computation.1 | async-start | bytes 8388608 | tf_op jit(solution)/shard_map/cond
  72.6 12.4 %copy-start = (bf16[1024,1024]{1,0:T(8,128)(2,1)S(1)}, bf16[1024,1024]{1,0:T(8,128)(2,1)}, u32[]{:S(2)}) copy-start(bf16[1024,1024]{1,0:T(8,128)(2,1)} %get-tuple-element.36) | copy-start | bytes 6291460 | tf_op jit(solution)/shard_map/cond
  72.6 21.7 %slice-start.4 = ((s8[6291456]{0:T(1024)(128)(4,1)}), s8[4194304]{0:T(1024)(128)(4,1)S(1)}, s32[]{:S(2)}) async-start(s8[6291456]{0:T(1024)(128)(4,1)} %bitcast.50), calls=%async_computation.4 | async-start | bytes 8388608 | tf_op jit(solution)/shard_map/cond
  82.5 201.7 %collective-permute-start.4 = (bf16[1792,1024]{1,0:T(8,128)(2,1)}, bf16[1792,1024]{1,0:T(8,128)(2,1)}, u32[]{:S(2)}, u32[]{:S(2)}) collective-permute-start(bf16[1792,1024]{1,0:T(8,128)(2,1)} %subtract_convert_fusion.1.refs_0_), channel_id=1, source_target_pairs={{0,8},{8,16},{16,24},{24,0},{1,9},{9,17},{17,25},{25,1},{2,10},{10... | collective-permute-start | bytes 11010056 | tf_op jit(solution)/shard_map/cond/branch_0_fun/ppermute | solution.py:323
  82.7 83.6 %collective-permute-start.8 = (bf16[1]{0:T(256)(128)(2,1)}, bf16[1]{0:T(256)(128)(2,1)}, u32[]{:S(2)}, u32[]{:S(2)}) collective-permute-start(bf16[1]{0:T(256)(128)(2,1)} %get-tuple-element.35), channel_id=1, source_target_pairs={{0,8},{8,16},{16,24},{24,0},{1,9},{9,17},{17,25},{25,1},{2,10},{10... | collective-permute-start | bytes 14 | tf_op jit(solution)/shard_map/cond/branch_0_fun/ppermute | solution.py:323
  85.0 9.3 %slice-start.5 = ((s8[6291456]{0:T(1024)(128)(4,1)}), s8[2097152]{0:T(1024)(128)(4,1)S(1)}, s32[]{:S(2)}) async-start(s8[6291456]{0:T(1024)(128)(4,1)} %bitcast.50), calls=%async_computation.5 | async-start | bytes 4194304 | tf_op jit(solution)/shard_map/cond
  85.0 9.3 %copy-start.3 = (bf16[1024,1024]{1,0:T(8,128)(2,1)S(1)}, bf16[1024,1024]{1,0:T(8,128)(2,1)}, u32[]{:S(2)}) copy-start(bf16[1024,1024]{1,0:T(8,128)(2,1)} %copy-done.2) | copy-start | bytes 6291460 | tf_op jit(solution)/shard_map/cond
  85.0 9.3 %copy-start.6 = (bf16[1024,2048]{1,0:T(8,128)(2,1)S(1)}, bf16[1024,2048]{1,0:T(8,128)(2,1)}, u32[]{:S(2)}) copy-start(bf16[1024,2048]{1,0:T(8,128)(2,1)} %rest_gather.5) | copy-start | bytes 12582916 | tf_op jit(solution)/shard_map/cond
  100.2 1.3 copy-start.16
  101.5 65.7 %copy-start.12 = (bf16[256,1024]{1,0:T(8,128)(2,1)}, bf16[256,1024]{1,0:T(8,128)(2,1)S(1)}, u32[]{:S(2)}) copy-start(bf16[256,1024]{1,0:T(8,128)(2,1)S(1)} %fusion.14.refs_0_) | copy-start | bytes 1572868 | tf_op jit(solution)/shard_map/cond
  166.3 117.9 %collective-permute-start.5 = (bf16[1792,1024]{1,0:T(8,128)(2,1)}, bf16[1792,1024]{1,0:T(8,128)(2,1)}, u32[]{:S(2)}, u32[]{:S(2)}) collective-permute-start(bf16[1792,1024]{1,0:T(8,128)(2,1)} %subtract_convert_fusion.refs_2_), channel_id=1, source_target_pairs={{0,8},{8,16},{16,24},{24,0},{1,9},{9,17},{17,25},{25,1},{2,10},{10... | collective-permute-start | bytes 11010056 | tf_op jit(solution)/shard_map/cond/branch_0_fun/ppermute | solution.py:323
  167.1 16.5 %copy-start.14 = (bf16[256,1024]{1,0:T(8,128)(2,1)}, bf16[256,1024]{1,0:T(8,128)(2,1)S(1)}, u32[]{:S(2)}) copy-start(bf16[256,1024]{1,0:T(8,128)(2,1)S(1)} %fusion.18.refs_2_) | copy-start | bytes 1572868 | tf_op jit(solution)/shard_map/cond
  167.1 111.6 %collective-permute-start.6 = (bf16[640,1024]{1,0:T(8,128)(2,1)}, bf16[640,1024]{1,0:T(8,128)(2,1)}, u32[]{:S(2)}, u32[]{:S(2)}) collective-permute-start(bf16[640,1024]{1,0:T(8,128)(2,1)} %subtract_convert_fusion.2.refs_0_), channel_id=1, source_target_pairs={{0,8},{8,16},{16,24},{24,0},{1,9},{9,17},{17,25},{25,1},{2,10},{10... | collective-permute-start | bytes 3932168 | tf_op jit(solution)/shard_map/cond/branch_0_fun/ppermute | solution.py:323
  167.2 129.4 %collective-permute-start.2 = (bf16[256,1024]{1,0:T(8,128)(2,1)S(1)}, bf16[256,1024]{1,0:T(8,128)(2,1)S(1)}, u32[]{:S(2)}, u32[]{:S(2)}) collective-permute-start(bf16[256,1024]{1,0:T(8,128)(2,1)S(1)} %fusion.14.refs_0_), channel_id=1, source_target_pairs={{0,8},{8,16},{16,24},{24,0},{1,9},{9,17},{17,25},{25,1},{2,10},{10... | collective-permute-start | bytes 1572872 | tf_op jit(solution)/shard_map/cond/branch_0_fun/ppermute | solution.py:323
  168.7 130.9 %collective-permute-start.3 = (bf16[256,1024]{1,0:T(8,128)(2,1)S(1)}, bf16[256,1024]{1,0:T(8,128)(2,1)}, u32[]{:S(2)}, u32[]{:S(2)}) collective-permute-start(bf16[256,1024]{1,0:T(8,128)(2,1)S(1)} %fusion.18.refs_2_), channel_id=1, source_target_pairs={{0,8},{8,16},{16,24},{24,0},{1,9},{9,17},{17,25},{25,1},{2,10},{10... | collective-permute-start | bytes 1572872 | tf_op jit(solution)/shard_map/cond/branch_0_fun/ppermute | solution.py:323
  183.5 73.0 %copy-start.10 = (bf16[384,1024]{1,0:T(8,128)(2,1)S(1)}, bf16[384,1024]{1,0:T(8,128)(2,1)}, u32[]{:S(2)}) copy-start(bf16[384,1024]{1,0:T(8,128)(2,1)} %get-tuple-element.32.refs_0_) | copy-start | bytes 2359300 | tf_op jit(solution)/shard_map/cond
  296.6 3.1 %copy-start.18 = (bf16[256,1024]{1,0:T(8,128)(2,1)}, bf16[256,1024]{1,0:T(8,128)(2,1)S(1)}, u32[]{:S(2)}) copy-start(bf16[256,1024]{1,0:T(8,128)(2,1)S(1)} %collective-permute-done.2.refs_1_) | copy-start | bytes 1572868 | tf_op jit(solution)/shard_map/cond
